TPU v7x, 512 devices: a whole 4x4x16 slice. The times are simulated.
512 devices in a mesh: dp: 16 (over z), tensor: 32 (over x, y, core).
Axes of the slice: x: 4, y: 4, z: 16, core: 2. Of those that a mesh axis runs over, the one named last changes fastest.
Arguments:
- pages: bfloat16 [2, 64, 64, 2048], P(None, 'dp', None, 'tensor'), may hold values from -8 to 8
- page_table: int32 [16, 2], replicated, may hold values from 0 to 63, as said below
- page_count: int32 [16], replicated, may hold values from 1 to 2
- last_len: int32 [16], replicated, may hold values from 1 to 64
- targets: int32 [16, 128], P('dp'), may hold values from 0 to 65535
- mix_key: float32 [2, 2048], P(None, 'tensor'), may hold values from 0.05 to 0.95
- w_key: bfloat16 [2, 2048, 8192], P(None, None, 'tensor'), may hold values from -0.125 to 0.125
- w_value: bfloat16 [2, 8192, 2048], P(None, 'tensor'), may hold values from -0.0625 to 0.0625
- ln_gain: float32 [2, 2048], replicated, may hold values from 0.5 to 1.5
- ln_bias: float32 [2, 2048], replicated, may hold values from -2 to 2
- head: bfloat16 [2, 2048, 65536], P(None, 'dp', 'tensor'), may hold values from -8 to 8
Outputs:
- token_logprob: float32 [16, 128], P('dp', 'tensor')
- ratio_sum: float32 [16], P('dp')
Inputs may be any that keep to these rules, and one draw needn't show every extreme that they name: Entries are distinct; the page lives on dp device page_table[r, p] // 4.
All inputs are finite; a program needn't handle non-finite values.
Results may differ from a plain program's by a relative error of at most 0.0029.
The roundings to bfloat16 on the way count: a program that leaves them out, or rounds other values in their place, can miss the bound.
Values may be sent and summed in bfloat16 or wider, within the bound.
A program may use at most 128 MiB of HBM per device.

v0:
```python
import jax
import jax.numpy as jnp
from jax import lax
from jax.sharding import PartitionSpec as P

D = 2048
epsilon = 1e-05


def joined(value, axis, join):
    pieces = jax.tree.map(lambda part: lax.all_gather(part, axis), value)
    head = jax.tree.map(lambda part: part[0], pieces)
    tail = jax.tree.map(lambda part: part[1:], pieces)
    total, _ = lax.scan(lambda total, piece: (join(total, piece), None), head, tail)
    return total


def combine(left_stats, right_stats):
    peak = jnp.maximum(left_stats[0], right_stats[0])
    totals = left_stats[1] * jnp.exp(left_stats[0] - peak) + right_stats[1] * jnp.exp(
        right_stats[0] - peak
    )
    return (peak, totals, left_stats[2] + right_stats[2])


def body(
    pages,
    page_table,
    page_count,
    last_len,
    targets,
    mix_key,
    w_key,
    w_value,
    ln_gain,
    ln_bias,
    head,
):
    tensor_count = lax.axis_size("tensor")
    owner = lax.axis_index("dp")
    tensor_index = lax.axis_index("tensor")
    page_len = pages.shape[2]
    width_local = pages.shape[3]
    page_cap = page_table.shape[1]
    slot_count = page_cap * page_len
    live_pages = jnp.arange(page_cap)[None, :] < page_count[:, None]
    table_row = page_table[owner]
    everything = lax.all_gather(pages, "dp", axis=1, tiled=True)
    states = jnp.take(everything, table_row, axis=1)
    states = jnp.where(live_pages[owner][None, :, None, None], states, jnp.zeros_like(states))
    states = states.reshape(2, slot_count, width_local)
    state_f = states.astype(jnp.float32)
    previous = jnp.concatenate(
        [jnp.zeros((2, 1, width_local), jnp.float32), state_f[:, :-1]], axis=1
    )
    shifted = (state_f + (previous - state_f) * mix_key[:, None, :]).astype(jnp.bfloat16)
    hidden = jnp.einsum(
        "msd,mdf->msf",
        lax.all_gather(shifted, "tensor", axis=2, tiled=True),
        w_key,
        preferred_element_type=jnp.float32,
    )
    key_act = (jnp.maximum(hidden, 0.0) ** 2).astype(jnp.bfloat16)
    partial_out = jnp.einsum("msf,mfd->msd", key_act, w_value, preferred_element_type=jnp.float32)
    ffn_out = lax.psum_scatter(partial_out, "tensor", scatter_dimension=2, tiled=True)
    residual = state_f + ffn_out
    row_sum, row_square = lax.psum(
        (jnp.sum(residual, axis=-1), jnp.sum(residual * residual, axis=-1)), "tensor"
    )
    average = row_sum / D
    variance = row_square / D - average * average
    gain_local = lax.dynamic_slice_in_dim(ln_gain, tensor_index * width_local, width_local, 1)
    bias_local = lax.dynamic_slice_in_dim(ln_bias, tensor_index * width_local, width_local, 1)
    normed_local = (
        (residual - average[..., None])
        * lax.rsqrt(variance + epsilon)[..., None]
        * gain_local[:, None, :]
        + bias_local[:, None, :]
    ).astype(jnp.bfloat16)
    normed = lax.all_gather(normed_local, "tensor", axis=2, tiled=True)
    vocab_local = head.shape[2]
    logits = jnp.einsum(
        "msd,mdv->msv",
        normed,
        lax.all_gather(head, "dp", axis=1, tiled=True),
        preferred_element_type=jnp.float32,
    )
    peak = jnp.max(logits, axis=-1)
    totals = jnp.sum(jnp.exp(logits - peak[..., None]), axis=-1)
    vocab_ids = jnp.arange(vocab_local) + tensor_index * vocab_local
    matches = vocab_ids[None, None, :] == targets[0][None, :, None]
    target_logit = jnp.sum(jnp.where(matches, logits, 0.0), axis=-1)
    peak, totals, target_logit = joined((peak, totals, target_logit), "tensor", combine)
    logp = target_logit - peak - jnp.log(totals)
    length = (page_count[owner] - 1) * page_len + last_len[owner]
    valid = jnp.arange(slot_count) < length
    policy_row = jnp.where(valid, logp[0], 0.0)
    ratio = jnp.sum(jnp.where(valid, logp[0] - logp[1], 0.0))
    share = slot_count // tensor_count
    token_part = lax.dynamic_slice_in_dim(policy_row, tensor_index * share, share)[None, :]
    return (token_part, ratio[None])


def solution(mesh):
    placed = (
        P(None, "dp", None, "tensor"),
        P(),
        P(),
        P(),
        P("dp", None),
        P(None, "tensor"),
        P(None, None, "tensor"),
        P(None, "tensor", None),
        P(),
        P(),
        P(None, "dp", "tensor"),
    )
    return jax.shard_map(
        body, mesh=mesh, in_specs=placed, out_specs=(P("dp", "tensor"), P("dp")), check_vma=False
    )
```

profile of v0, /device:TPU:1, one launch (start us, length us, event | category | flops | bytes accessed | tf_op | source)
XLA Modules:
  0.0 654.3 jit_solution(647617080670465465)
XLA Ops:
  7.2 0.0 copy-start
  7.2 0.0 all-gather.11.cloned.1.call-start
  7.2 0.7 all-gather.11.cloned.1.call-update
  7.9 0.0 all-gather.13.cloned.1.call-start
  8.0 0.9 dynamic-slice_reduce_fusion
  8.8 1.2 dynamic_slice.31
  10.1 0.7 compare_bitcast_fusion
  10.7 0.1 broadcast_in_dim.65
  10.8 0.1 broadcast_in_dim.66
  10.9 0.1 broadcast_in_dim.68
  11.0 0.1 broadcast_in_dim.69
  11.1 68.5 %all-gather.11.cloned.1.call-done = bf16[2,64,64,64]{3,2,1,0:T(8,128)(2,1)} async-done(((bf16[2,4,64,64]{3,2,1,0:T(8,128)(2,1)}), bf16[2,64,64,64]{3,2,1,0:T(8,128)(2,1)}) %all-gather.11.cloned.1.call-update) | async-done | bytes 1048592 | tf_op jit(solution)/shard_map/all_gather | solution.py:48
  79.6 2.2 gather_fusion
  81.7 0.1 copy.15
  81.8 0.1 gather.7
  81.9 1.4 add_convert_fusion.1
  83.3 0.0 all-gather.13.cloned.1.call-update
  83.4 0.0 reduce-scatter.2.cloned.1.call-start
  83.4 64.8 %all-gather.13.cloned.1.call-done = bf16[2,128,2048]{1,2,0:T(8,128)(2,1)} async-done(((bf16[2,128,64]{1,2,0:T(8,128)(2,1)}), bf16[2,128,2048]{1,2,0:T(8,128)(2,1)}) %all-gather.13.cloned.1.call-update) | async-done | bytes 1048592 | tf_op jit(solution)/shard_map/all_gather | solution.py:59
  148.2 0.0 copy-done
  148.2 4.5 fusion.4
  152.7 0.0 copy-start.2
  152.7 0.0 copy-start.1
  152.7 0.0 reduce-scatter.2.cloned.1.call-update
  152.7 0.0 all-gather.15.cloned.1.call-start
  152.8 0.8 constant_dynamic-slice_fusion.1
  153.6 98.6 %reduce-scatter.2.cloned.1.call-done = f32[2,128,64]{1,2,0:T(8,128)} async-done(((f32[2,128,2048]{1,2,0:T(8,128)}), f32[2,128,64]{1,2,0:T(8,128)}) %reduce-scatter.2.cloned.1.call-update) | async-done | bytes 65552 | tf_op jit(solution)/shard_map/reduce_scatter | solution.py:65
  252.1 0.9 fusion.6
  253.0 64.3 %all-reduce.1 = (f32[2,128]{1,0:T(2,128)S(1)}, f32[2,128]{1,0:T(2,128)S(1)}) all-reduce(f32[2,128]{1,0:T(2,128)S(1)} %get-tuple-element.47, f32[2,128]{1,0:T(2,128)S(1)} %get-tuple-element.46), channel_id=1, replica_groups=mesh['dp'=16,'tensor'=32] {'tensor'}, use_global_device_ids=true, to_apply=%region_4.5 | all-reduce | flops 512 | bytes 4096 | tf_op jit(solution)/shard_map/psum | solution.py:67
  317.3 1.6 add_convert_fusion
  318.9 0.0 all-gather.15.cloned.1.call-update
  318.9 0.0 all-gather.17.cloned.1.call-start
  319.0 0.5 all-gather.17.cloned.1.call-update
  320.2 0.0 copy-done.2
  320.2 0.6 dynamic_slice.32
  321.4 0.0 copy-done.1
  321.4 0.2 broadcast_compare_fusion
  321.7 53.0 %all-gather.15.cloned.1.call-done = bf16[2,128,2048]{1,2,0:T(8,128)(2,1)} async-done(((bf16[2,128,64]{1,2,0:T(8,128)(2,1)}), bf16[2,128,2048]{1,2,0:T(8,128)(2,1)}) %all-gather.15.cloned.1.call-update) | async-done | bytes 1048592 | tf_op jit(solution)/shard_map/all_gather | solution.py:80
  374.6 191.1 %all-gather.17.cloned.1.call-done = bf16[2,2048,2048]{2,1,0:T(8,128)(2,1)} async-done(((bf16[2,128,2048]{2,1,0:T(8,128)(2,1)}), bf16[2,2048,2048]{2,1,0:T(8,128)(2,1)}) %all-gather.17.cloned.1.call-update) | async-done | bytes 16777232 | tf_op jit(solution)/shard_map/all_gather | solution.py:85
  565.7 8.6 %fusion.11 = (f32[2,128]{1,0:T(2,128)S(1)}, f32[2,128,2048]{2,1,0:T(8,128)S(1)}) fusion(bf16[2,128,2048]{1,2,0:T(8,128)(2,1)} %all-gather.15.cloned.1.call-done, bf16[2,2048,2048]{2,1,0:T(8,128)(2,1)} %all-gather.17.cloned.1.call-done), kind=kOutput, calls=%fused_computation.45 | convolution fusion | flops 2148007680 | bytes 19923968 | tf_op jit(solution)/shard_map/msd,mdv->msv/dot_general | solution.py:82
  574.4 0.7 select_reduce_fusion
  575.1 24.7 %all-gather.5 = f32[32,2,128]{2,1,0:T(2,128)S(1)} all-gather(f32[1,2,128]{2,1,0:T(2,128)S(1)} %bitcast.56), channel_id=4, replica_groups=mesh['dp'=16,'tensor'=32] {'tensor'}, dimensions={0}, use_global_device_ids=true | all-gather | bytes 33792 | tf_op jit(solution)/shard_map/all_gather | solution.py:11
  599.8 23.5 %all-gather.4 = f32[32,2,128]{2,1,0:T(2,128)S(1)} all-gather(f32[1,2,128]{2,1,0:T(2,128)S(1)} %bitcast.55), channel_id=3, replica_groups=mesh['dp'=16,'tensor'=32] {'tensor'}, dimensions={0}, use_global_device_ids=true | all-gather | bytes 33792 | tf_op jit(solution)/shard_map/all_gather | solution.py:11
  623.3 21.9 %all-gather.3 = f32[32,2,128]{2,1,0:T(2,128)S(1)} all-gather(f32[1,2,128]{2,1,0:T(2,128)S(1)} %bitcast.54), channel_id=2, replica_groups=mesh['dp'=16,'tensor'=32] {'tensor'}, dimensions={0}, use_global_device_ids=true | all-gather | bytes 33792 | tf_op jit(solution)/shard_map/all_gather | solution.py:11
  645.2 1.3 while.14
  646.5 0.6 fusion.7
  647.1 0.6 dynamic-slice_bitcast_fusion
  (44 shorter events, 1.0 us)
Async XLA Ops:
  7.2 141.0 %copy-start = (bf16[2,256,2048]{2,1,0:T(8,128)(2,1)S(1)}, bf16[2,256,2048]{2,1,0:T(8,128)(2,1)}, u32[]{:S(2)}) copy-start(bf16[2,256,2048]{2,1,0:T(8,128)(2,1)} %param.20) | copy-start | bytes 6291460
  7.2 72.4 %all-gather.11.cloned.1.call-start = ((), (), s32[]{:S(2)}) async-start(), calls=%async_computation.1 | async-start | bytes 2228224 | tf_op jit(solution)/shard_map/all_gather | solution.py:48
  7.9 140.3 %all-gather.13.cloned.1.call-start = ((), (), s32[]{:S(2)}) async-start(), calls=%async_computation.2 | async-start | bytes 1081344 | tf_op jit(solution)/shard_map/all_gather | solution.py:59
  83.4 168.8 %reduce-scatter.2.cloned.1.call-start = ((), (), s32[]{:S(2)}) async-start(), calls=%async_computation.3 | async-start | bytes 2162688 | tf_op jit(solution)/shard_map/reduce_scatter | solution.py:65
  152.7 167.5 %copy-start.2 = (s32[16]{0:T(128)S(1)}, s32[16]{0:T(128)}, u32[]{:S(2)}) copy-start(s32[16]{0:T(128)} %param.16) | copy-start | bytes 196
  152.7 168.7 %copy-start.1 = (s32[1,128]{1,0:T(1,128)S(1)}, s32[1,128]{1,0:T(1,128)}, u32[]{:S(2)}) copy-start(s32[1,128]{1,0:T(1,128)} %param.17) | copy-start | bytes 1540
  152.7 221.9 %all-gather.15.cloned.1.call-start = ((), (), s32[]{:S(2)}) async-start(), calls=%async_computation.4 | async-start | bytes 1081344 | tf_op jit(solution)/shard_map/all_gather | solution.py:80
  318.9 246.8 %all-gather.17.cloned.1.call-start = ((), (), s32[]{:S(2)}) async-start(), calls=%async_computation.5 | async-start | bytes 17825792 | tf_op jit(solution)/shard_map/all_gather | solution.py:85
Sparse Core Ops, SparseCore 0:
  10.1 69.4 all-gather.10
  83.5 64.6 all-gather.12
  152.9 99.2 reduce-scatter.1
  319.0 55.5 all-gather.14
  376.5 189.1 all-gather.16
where the time goes:
time: 655 us; the launch traced here: 654 us
  waiting for transfers between devices  477 us (73%)
  blocking collectives  134 us (20%)
  between operations  15.2 us (2%)
  matrix products  13.2 us (2%)
  other arithmetic  6.97 us (1%)
  local copies, waits for them, and re-layouts  6.76 us (1%)
    all_gather x1, waiting for transfers between devices, body(): lax.all_gather(head, 'dp', axis=1, tiled=True)  191 us
    reduce_scatter x1, waiting for transfers between devices, body(): lax.psum_scatter(partial_out, 'tensor', scatter_dimension=2, tiled=True)  98.6 us
    all_gather x3, blocking collectives, joined(): pieces = jax.tree.map(lambda part: lax.all_gather(part, axis), value)  70.1 us
    all_gather x1, waiting for transfers between devices, body(): everything = lax.all_gather(pages, 'dp', axis=1, tiled=True)  68.5 us
    all_gather x1, waiting for transfers between devices, body(): lax.all_gather(shifted, 'tensor', axis=2, tiled=True)  64.8 us
    psum x1, blocking collectives, body(): lax.psum((jnp.sum(residual, axis=-1), jnp.sum(residual * residual, axis=-...  64.3 us
    all_gather x1, waiting for transfers between devices, body(): normed = lax.all_gather(normed_local, 'tensor', axis=2, tiled=True)  53 us
  transfers between devices with their start and end apart: 5, of which 5 were waited for; matrix products, arithmetic and copies ran while one was open for 1% of the time, Pallas kernels for 0%

commit v1 on v0

--- a/solution.py
+++ b/solution.py
@@ -1,3 +1,4 @@
+import functools
 import jax
 import jax.numpy as jnp
 from jax import lax
@@ -5,6 +6,35 @@
 
 D = 2048
 epsilon = 1e-05
+
+
+def load_the_values(matrix, d0):
+    value_now = list(matrix.shape[1:])
+    value_now[d0] *= matrix.shape[0]
+    return jnp.moveaxis(matrix, 0, d0).reshape(value_now)
+
+
+def pass_the_field(sample, lane_axis, join_dim):
+    n_peers_all = lax.axis_size(lane_axis)
+    seen = [(src_i, (src_i + 1) % n_peers_all) for src_i in range(n_peers_all)]
+    windows = [(h, num) for num, h in seen]
+    q_next, y = ([], [])
+    for ix in range(n_peers_all - 1):
+        if ix % 2 == 0:
+            ready = lax.ppermute(q_next[-1] if q_next else sample, perm=seen, axis_name=lane_axis)
+            q_next.append(ready)
+        else:
+            part_next = lax.ppermute(y[-1] if y else sample, axis_name=lane_axis, perm=windows)
+            y.append(part_next)
+    outer = jnp.stack([*q_next[::-1], sample, *y])
+    small = lax.axis_index(lane_axis)
+    carry_out = len(q_next)
+    latest = small - carry_out
+    outer = outer[(jnp.arange(n_peers_all) - latest) % n_peers_all]
+    return load_the_values(outer, join_dim)
+
+
+_keep_up_region = functools.partial(pass_the_field, lane_axis="dp", join_dim=1)
 
 
 def joined(value, axis, join):
@@ -80,10 +110,7 @@
     normed = lax.all_gather(normed_local, "tensor", axis=2, tiled=True)
     vocab_local = head.shape[2]
     logits = jnp.einsum(
-        "msd,mdv->msv",
-        normed,
-        lax.all_gather(head, "dp", axis=1, tiled=True),
-        preferred_element_type=jnp.float32,
+        "msd,mdv->msv", normed, _keep_up_region(head), preferred_element_type=jnp.float32
     )
     peak = jnp.max(logits, axis=-1)
     totals = jnp.sum(jnp.exp(logits - peak[..., None]), axis=-1)

time: 655 us -> 475 us (0.73)
  waiting for transfers between devices: 477 us -> 179 us
  local copies, waits for them, and re-layouts: 6.76 us -> 68.3 us
  starting transfers between devices: 0.2 us -> 58 us
    all_gather x1 -> x0, waiting for transfers between devices: 191 us -> none  [body(): lax.all_gather(head, 'dp', axis=1, tiled=True)]
    ppermute x0 -> x15, waiting for transfers between devices: none -> 96.6 us  [the longest x8 96.5 us: pass_the_field(): lax.ppermute(q_next[-1] if q_next else sample, perm=seen, axis_name=lane_...]
    reduce_scatter x1, waiting for transfers between devices: 98.6 us -> 35 us  [body(): lax.psum_scatter(partial_out, 'tensor', scatter_dimension=2, tiled=True)]
    ppermute x0 -> x15, starting transfers between devices: none -> 57.8 us  [the longest x7 38.7 us: pass_the_field(): lax.ppermute(y[-1] if y else sample, axis_name=lane_axis, perm=windows)]
    all_gather x1, waiting for transfers between devices: 53 us -> 0.01 us  [body(): normed = lax.all_gather(normed_local, 'tensor', axis=2, tiled=True)]
    all_gather x1, waiting for transfers between devices: 64.8 us -> 15.2 us  [body(): lax.all_gather(shifted, 'tensor', axis=2, tiled=True)]
    all_gather x1, waiting for transfers between devices: 68.5 us -> 31 us  [body(): everything = lax.all_gather(pages, 'dp', axis=1, tiled=True)]
    unnamed x6 -> x21, local copies, waits for them, and re-layouts: 0.02 us -> 31.2 us
  transfers between devices with their start and end apart: 5 -> 19, of which waited for: 5 -> 8; matrix products, arithmetic and copies ran while one was open for 1% -> 16% of each run, Pallas kernels for 0% -> 0%
where the time goes in v1:
time: 475 us; the launch traced here: 473 us
  waiting for transfers between devices  179 us (38%)
  blocking collectives  132 us (28%)
  local copies, waits for them, and re-layouts  68.3 us (14%)
  starting transfers between devices  58 us (12%)
  between operations  15.4 us (3%)
  matrix products  13.1 us (3%)
  other arithmetic  7.63 us (2%)
    ppermute x8, waiting for transfers between devices, pass_the_field(): lax.ppermute(q_next[-1] if q_next else sample, perm=seen, axis_name=lane_...  96.5 us
    all_gather x3, blocking collectives, joined(): pieces = jax.tree.map(lambda part: lax.all_gather(part, axis), value)  67.8 us
    psum x1, blocking collectives, body(): lax.psum((jnp.sum(residual, axis=-1), jnp.sum(residual * residual, axis=-...  64.3 us
    ppermute x7, starting transfers between devices, pass_the_field(): lax.ppermute(y[-1] if y else sample, axis_name=lane_axis, perm=windows)  38.7 us
    reduce_scatter x1, waiting for transfers between devices, body(): lax.psum_scatter(partial_out, 'tensor', scatter_dimension=2, tiled=True)  35 us
    unnamed x21, local copies, waits for them, and re-layouts  31.2 us
    all_gather x1, waiting for transfers between devices, body(): everything = lax.all_gather(pages, 'dp', axis=1, tiled=True)  31 us
    ppermute x8, starting transfers between devices, pass_the_field(): lax.ppermute(q_next[-1] if q_next else sample, perm=seen, axis_name=lane_...  19.2 us
  transfers between devices with their start and end apart: 19, of which 8 were waited for; matrix products, arithmetic and copies ran while one was open for 16% of the time, Pallas kernels for 0%

profile of v1, /device:TPU:1, one launch (start us, length us, event | category | flops | bytes accessed | tf_op | source)
XLA Modules:
  0.0 473.5 jit_solution(10213361912767682947)
XLA Ops:
  8.0 4.5 collective-permute-start
  12.5 9.5 %collective-permute-start.8 = (bf16[2,128,2048]{2,1,0:T(8,128)(2,1)}, bf16[2,128,2048]{2,1,0:T(8,128)(2,1)}, u32[]{:S(2)}, u32[]{:S(2)}) collective-permute-start(bf16[2,128,2048]{2,1,0:T(8,128)(2,1)} %param.23), channel_id=1, source_target_pairs={{32,0},{64,32},{96,64},{128,96},{160,128},{192,160},{224,192},{256... | collective-permute-start | bytes 3145736 | tf_op jit(solution)/shard_map/ppermute | solution.py:27
  22.0 25.6 %collective-permute-done = bf16[2,128,2048]{2,1,0:T(8,128)(2,1)} collective-permute-done((bf16[2,128,2048]{2,1,0:T(8,128)(2,1)}, bf16[2,128,2048]{2,1,0:T(8,128)(2,1)}, u32[]{:S(2)}, u32[]{:S(2)}) %collective-permute-start) | collective-permute-done | bytes 1048608 | tf_op jit(solution)/shard_map/ppermute | solution.py:24
  47.6 1.9 collective-permute-start.1
  52.7 4.6 collective-permute-start.9
  57.3 31.0 %all-gather.10.cloned.1.call-done = bf16[2,64,64,64]{3,2,1,0:T(8,128)(2,1)} async-done(((bf16[2,4,64,64]{3,2,1,0:T(8,128)(2,1)}), bf16[2,64,64,64]{3,2,1,0:T(8,128)(2,1)}) %all-gather.10.cloned.1.call-update) | async-done | bytes 1048592 | tf_op jit(solution)/shard_map/all_gather | solution.py:78
  88.3 2.2 gather_fusion
  90.7 1.9 collective-permute-start.2
  92.6 1.4 add_convert_fusion.1
  94.1 18.2 %collective-permute-done.2 = bf16[2,128,2048]{2,1,0:T(8,128)(2,1)} collective-permute-done((bf16[2,128,2048]{2,1,0:T(8,128)(2,1)}, bf16[2,128,2048]{2,1,0:T(8,128)(2,1)}, u32[]{:S(2)}, u32[]{:S(2)}) %collective-permute-start.2) | collective-permute-done | bytes 1048608 | tf_op jit(solution)/shard_map/ppermute | solution.py:24
  112.3 1.9 collective-permute-start.3
  114.2 4.6 collective-permute-start.10
  118.8 15.1 %collective-permute-done.3 = bf16[2,128,2048]{2,1,0:T(8,128)(2,1)} collective-permute-done((bf16[2,128,2048]{2,1,0:T(8,128)(2,1)}, bf16[2,128,2048]{2,1,0:T(8,128)(2,1)}, u32[]{:S(2)}, u32[]{:S(2)}) %collective-permute-start.3) | collective-permute-done | bytes 1048608 | tf_op jit(solution)/shard_map/ppermute | solution.py:24
  133.9 1.9 collective-permute-start.4
  135.8 4.6 collective-permute-start.11
  140.4 15.2 %all-gather.12.cloned.1.call-done = bf16[2,128,2048]{1,2,0:T(8,128)(2,1)} async-done(((bf16[2,128,64]{1,2,0:T(8,128)(2,1)}), bf16[2,128,2048]{1,2,0:T(8,128)(2,1)}) %all-gather.12.cloned.1.call-update) | async-done | bytes 1048592 | tf_op jit(solution)/shard_map/all_gather | solution.py:89
  155.7 4.5 fusion.4
  160.3 3.2 collective-permute-start.5
  163.5 4.4 collective-permute-start.12
  167.9 18.3 %collective-permute-done.5 = bf16[2,128,2048]{2,1,0:T(8,128)(2,1)} collective-permute-done((bf16[2,128,2048]{2,1,0:T(8,128)(2,1)}, bf16[2,128,2048]{2,1,0:T(8,128)(2,1)}, u32[]{:S(2)}, u32[]{:S(2)}) %collective-permute-start.5) | collective-permute-done | bytes 1048608 | tf_op jit(solution)/shard_map/ppermute | solution.py:24
  186.2 1.9 collective-permute-start.6
  188.1 6.5 %collective-permute-start.13 = (bf16[2,128,2048]{2,1,0:T(8,128)(2,1)S(1)}, bf16[2,128,2048]{2,1,0:T(8,128)(2,1)S(1)}, u32[]{:S(2)}, u32[]{:S(2)}) collective-permute-start(bf16[2,128,2048]{2,1,0:T(8,128)(2,1)S(1)} %collective-permute-done.12), channel_id=1, source_target_pairs={{32,0},{64,32},{96,64},{128,96},{160,128},{192,160},{224,192},{256... | collective-permute-start | bytes 3145736 | tf_op jit(solution)/shard_map/ppermute | solution.py:27
  194.7 19.2 %collective-permute-done.6 = bf16[2,128,2048]{2,1,0:T(8,128)(2,1)} collective-permute-done((bf16[2,128,2048]{2,1,0:T(8,128)(2,1)}, bf16[2,128,2048]{2,1,0:T(8,128)(2,1)}, u32[]{:S(2)}, u32[]{:S(2)}) %collective-permute-start.6) | collective-permute-done | bytes 1048608 | tf_op jit(solution)/shard_map/ppermute | solution.py:24
  213.9 1.9 collective-permute-start.7
  220.0 4.6 collective-permute-start.14
  224.6 35.0 %reduce-scatter.2.cloned.1.call-done = f32[2,128,64]{1,2,0:T(8,128)} async-done(((f32[2,128,2048]{1,2,0:T(8,128)}), f32[2,128,64]{1,2,0:T(8,128)}) %reduce-scatter.2.cloned.1.call-update) | async-done | bytes 65552 | tf_op jit(solution)/shard_map/reduce_scatter | solution.py:95
  260.5 64.3 %all-reduce.1 = (f32[2,128]{1,0:T(2,128)S(1)}, f32[2,128]{1,0:T(2,128)S(1)}) all-reduce(f32[2,128]{1,0:T(2,128)S(1)} %get-tuple-element.47, f32[2,128]{1,0:T(2,128)S(1)} %get-tuple-element.46), channel_id=1, replica_groups=mesh['dp'=16,'tensor'=32] {'tensor'}, use_global_device_ids=true, to_apply=%region_4.5 | all-reduce | flops 512 | bytes 4096 | tf_op jit(solution)/shard_map/psum | solution.py:97
  324.8 1.6 add_convert_fusion
  326.4 2.3 bitcast_dynamic-update-slice_fusion.15
  328.7 2.3 bitcast_dynamic-update-slice_fusion.14
  331.0 2.3 bitcast_dynamic-update-slice_fusion.13
  333.3 2.3 bitcast_dynamic-update-slice_fusion.12
  335.7 2.3 bitcast_dynamic-update-slice_fusion.11
  338.0 2.3 bitcast_dynamic-update-slice_fusion.10
  340.3 2.3 bitcast_dynamic-update-slice_fusion.9
  342.6 2.3 bitcast_dynamic-update-slice_fusion.8
  346.1 2.3 bitcast_dynamic-update-slice_fusion.6
  348.4 2.3 bitcast_dynamic-update-slice_fusion.5
  350.7 2.3 bitcast_dynamic-update-slice_fusion.4
  353.0 2.4 bitcast_dynamic-update-slice_fusion.3
  357.6 2.3 bitcast_dynamic-update-slice_fusion
  359.9 13.1 %gather_fusion.1 = bf16[16,2,128,2048]{3,2,1,0:T(8,128)(2,1)} fusion(bf16[16,2,128,2048]{3,2,1,0:T(8,128)(2,1)} %bitcast_dynamic-update-slice_fusion, s32[1024]{0:T(1024)S(1)} %pad_clamp_fusion), kind=kCustom, calls=%fused_computation.1 | custom fusion | bytes 33554496 | tf_op jit(solution)/shard_map/gather | solution.py:33
  373.0 14.2 %copy.22 = bf16[2,16,128,2048]{3,2,1,0:T(8,128)(2,1)} copy(bf16[2,16,128,2048]{3,2,0,1:T(8,128)(2,1)} %bitcast.89) | data formatting | bytes 33554432 | tf_op jit(solution)/shard_map/transpose | solution.py:14
  387.2 8.6 %fusion.13 = (f32[2,128]{1,0:T(2,128)S(1)}, f32[2,128,2048]{2,1,0:T(8,128)S(1)}) fusion(bf16[2,128,2048]{1,2,0:T(8,128)(2,1)} %all-gather.14.cloned.1.call-done, bf16[2,2048,2048]{2,1,0:T(8,128)(2,1)} %bitcast.88), kind=kOutput, calls=%fused_computation.69 | convolution fusion | flops 2148007680 | bytes 19923968 | tf_op jit(solution)/shard_map/msd,mdv->msv/dot_general | solution.py:112
  396.6 21.3 %all-gather.5 = f32[32,2,128]{2,1,0:T(2,128)S(1)} all-gather(f32[1,2,128]{2,1,0:T(2,128)S(1)} %bitcast.94), channel_id=4, replica_groups=mesh['dp'=16,'tensor'=32] {'tensor'}, dimensions={0}, use_global_device_ids=true | all-gather | bytes 33792 | tf_op jit(solution)/shard_map/all_gather | solution.py:41
  417.9 25.1 %all-gather.4 = f32[32,2,128]{2,1,0:T(2,128)S(1)} all-gather(f32[1,2,128]{2,1,0:T(2,128)S(1)} %bitcast.93), channel_id=3, replica_groups=mesh['dp'=16,'tensor'=32] {'tensor'}, dimensions={0}, use_global_device_ids=true | all-gather | bytes 33792 | tf_op jit(solution)/shard_map/all_gather | solution.py:41
  443.0 21.4 %all-gather.3 = f32[32,2,128]{2,1,0:T(2,128)S(1)} all-gather(f32[1,2,128]{2,1,0:T(2,128)S(1)} %bitcast.92), channel_id=2, replica_groups=mesh['dp'=16,'tensor'=32] {'tensor'}, dimensions={0}, use_global_device_ids=true | all-gather | bytes 33792 | tf_op jit(solution)/shard_map/all_gather | solution.py:41
  464.4 1.3 while.14
  (90 shorter events, 14.2 us)
Async XLA Ops:
  7.2 148.5 %copy-start = (bf16[2,256,2048]{2,1,0:T(8,128)(2,1)S(1)}, bf16[2,256,2048]{2,1,0:T(8,128)(2,1)}, u32[]{:S(2)}) copy-start(bf16[2,256,2048]{2,1,0:T(8,128)(2,1)} %param.20) | copy-start | bytes 6291460
  7.2 337.8 %copy-start.2 = (bf16[2,128,2048]{2,1,0:T(8,128)(2,1)S(1)}, bf16[2,128,2048]{2,1,0:T(8,128)(2,1)}, u32[]{:S(2)}) copy-start(bf16[2,128,2048]{2,1,0:T(8,128)(2,1)} %param.23) | copy-start | bytes 3145732
  7.2 81.1 %all-gather.10.cloned.1.call-start = ((), (), s32[]{:S(2)}) async-start(), calls=%async_computation.1 | async-start | bytes 2228224 | tf_op jit(solution)/shard_map/all_gather | solution.py:78
  7.9 147.7 %all-gather.12.cloned.1.call-start = ((), (), s32[]{:S(2)}) async-start(), calls=%async_computation.2 | async-start | bytes 1081344 | tf_op jit(solution)/shard_map/all_gather | solution.py:89
  8.0 39.7 %collective-permute-start = (bf16[2,128,2048]{2,1,0:T(8,128)(2,1)}, bf16[2,128,2048]{2,1,0:T(8,128)(2,1)}, u32[]{:S(2)}, u32[]{:S(2)}) collective-permute-start(bf16[2,128,2048]{2,1,0:T(8,128)(2,1)} %param.23), channel_id=1, source_target_pairs={{0,32},{32,64},{64,96},{96,128},{128,160},{160,192},{192,224},{224... | collective-permute-start | bytes 3145736 | tf_op jit(solution)/shard_map/ppermute | solution.py:24
  12.5 40.2 %collective-permute-start.8 = (bf16[2,128,2048]{2,1,0:T(8,128)(2,1)}, bf16[2,128,2048]{2,1,0:T(8,128)(2,1)}, u32[]{:S(2)}, u32[]{:S(2)}) collective-permute-start(bf16[2,128,2048]{2,1,0:T(8,128)(2,1)} %param.23), channel_id=1, source_target_pairs={{32,0},{64,32},{96,64},{128,96},{160,128},{192,160},{224,192},{256... | collective-permute-start | bytes 3145736 | tf_op jit(solution)/shard_map/ppermute | solution.py:27
  47.6 43.0 %collective-permute-start.1 = (bf16[2,128,2048]{2,1,0:T(8,128)(2,1)}, bf16[2,128,2048]{2,1,0:T(8,128)(2,1)}, u32[]{:S(2)}, u32[]{:S(2)}) collective-permute-start(bf16[2,128,2048]{2,1,0:T(8,128)(2,1)} %collective-permute-done), channel_id=1, source_target_pairs={{0,32},{32,64},{64,96},{96,128},{128,160},{160,192},{192,224},{224... | collective-permute-start | bytes 3145736 | tf_op jit(solution)/shard_map/ppermute | solution.py:24
  52.7 61.5 %collective-permute-start.9 = (bf16[2,128,2048]{2,1,0:T(8,128)(2,1)}, bf16[2,128,2048]{2,1,0:T(8,128)(2,1)}, u32[]{:S(2)}, u32[]{:S(2)}) collective-permute-start(bf16[2,128,2048]{2,1,0:T(8,128)(2,1)} %collective-permute-done.8), channel_id=1, source_target_pairs={{32,0},{64,32},{96,64},{128,96},{160,128},{192,160},{224,192},{256... | collective-permute-start | bytes 3145736 | tf_op jit(solution)/shard_map/ppermute | solution.py:27
  90.7 21.6 %collective-permute-start.2 = (bf16[2,128,2048]{2,1,0:T(8,128)(2,1)}, bf16[2,128,2048]{2,1,0:T(8,128)(2,1)}, u32[]{:S(2)}, u32[]{:S(2)}) collective-permute-start(bf16[2,128,2048]{2,1,0:T(8,128)(2,1)} %collective-permute-done.1), channel_id=1, source_target_pairs={{0,32},{32,64},{64,96},{96,128},{128,160},{160,192},{192,224},{224... | collective-permute-start | bytes 3145736 | tf_op jit(solution)/shard_map/ppermute | solution.py:24
  94.0 165.6 %reduce-scatter.2.cloned.1.call-start = ((), (), s32[]{:S(2)}) async-start(), calls=%async_computation.3 | async-start | bytes 2162688 | tf_op jit(solution)/shard_map/reduce_scatter | solution.py:95
  112.3 21.6 %collective-permute-start.3 = (bf16[2,128,2048]{2,1,0:T(8,128)(2,1)}, bf16[2,128,2048]{2,1,0:T(8,128)(2,1)}, u32[]{:S(2)}, u32[]{:S(2)}) collective-permute-start(bf16[2,128,2048]{2,1,0:T(8,128)(2,1)} %collective-permute-done.2), channel_id=1, source_target_pairs={{0,32},{32,64},{64,96},{96,128},{128,160},{160,192},{192,224},{224... | collective-permute-start | bytes 3145736 | tf_op jit(solution)/shard_map/ppermute | solution.py:24
  114.2 21.6 %collective-permute-start.10 = (bf16[2,128,2048]{2,1,0:T(8,128)(2,1)}, bf16[2,128,2048]{2,1,0:T(8,128)(2,1)}, u32[]{:S(2)}, u32[]{:S(2)}) collective-permute-start(bf16[2,128,2048]{2,1,0:T(8,128)(2,1)} %collective-permute-done.9), channel_id=1, source_target_pairs={{32,0},{64,32},{96,64},{128,96},{160,128},{192,160},{224,192},{256... | collective-permute-start | bytes 3145736 | tf_op jit(solution)/shard_map/ppermute | solution.py:27
  133.9 26.3 %collective-permute-start.4 = (bf16[2,128,2048]{2,1,0:T(8,128)(2,1)}, bf16[2,128,2048]{2,1,0:T(8,128)(2,1)}, u32[]{:S(2)}, u32[]{:S(2)}) collective-permute-start(bf16[2,128,2048]{2,1,0:T(8,128)(2,1)} %collective-permute-done.3), channel_id=1, source_target_pairs={{0,32},{32,64},{64,96},{96,128},{128,160},{160,192},{192,224},{224... | collective-permute-start | bytes 3145736 | tf_op jit(solution)/shard_map/ppermute | solution.py:24
  135.8 27.6 %collective-permute-start.11 = (bf16[2,128,2048]{2,1,0:T(8,128)(2,1)}, bf16[2,128,2048]{2,1,0:T(8,128)(2,1)}, u32[]{:S(2)}, u32[]{:S(2)}) collective-permute-start(bf16[2,128,2048]{2,1,0:T(8,128)(2,1)} %collective-permute-done.10), channel_id=1, source_target_pairs={{32,0},{64,32},{96,64},{128,96},{160,128},{192,160},{224,192},{256... | collective-permute-start | bytes 3145736 | tf_op jit(solution)/shard_map/ppermute | solution.py:27
  160.2 227.0 %all-gather.14.cloned.1.call-start = ((), (), s32[]{:S(2)}) async-start(), calls=%async_computation.4 | async-start | bytes 1081344 | tf_op jit(solution)/shard_map/all_gather | solution.py:110
  160.3 25.9 %collective-permute-start.5 = (bf16[2,128,2048]{2,1,0:T(8,128)(2,1)}, bf16[2,128,2048]{2,1,0:T(8,128)(2,1)}, u32[]{:S(2)}, u32[]{:S(2)}) collective-permute-start(bf16[2,128,2048]{2,1,0:T(8,128)(2,1)} %collective-permute-done.4), channel_id=1, source_target_pairs={{0,32},{32,64},{64,96},{96,128},{128,160},{160,192},{192,224},{224... | collective-permute-start | bytes 3145736 | tf_op jit(solution)/shard_map/ppermute | solution.py:24
  163.5 24.7 %collective-permute-start.12 = (bf16[2,128,2048]{2,1,0:T(8,128)(2,1)}, bf16[2,128,2048]{2,1,0:T(8,128)(2,1)S(1)}, u32[]{:S(2)}, u32[]{:S(2)}) collective-permute-start(bf16[2,128,2048]{2,1,0:T(8,128)(2,1)} %collective-permute-done.11), channel_id=1, source_target_pairs={{32,0},{64,32},{96,64},{128,96},{160,128},{192,160},{224,192},{256... | collective-permute-start | bytes 3145736 | tf_op jit(solution)/shard_map/ppermute | solution.py:27
  186.2 27.7 %collective-permute-start.6 = (bf16[2,128,2048]{2,1,0:T(8,128)(2,1)}, bf16[2,128,2048]{2,1,0:T(8,128)(2,1)}, u32[]{:S(2)}, u32[]{:S(2)}) collective-permute-start(bf16[2,128,2048]{2,1,0:T(8,128)(2,1)} %collective-permute-done.5), channel_id=1, source_target_pairs={{0,32},{32,64},{64,96},{96,128},{128,160},{160,192},{192,224},{224... | collective-permute-start | bytes 3145736 | tf_op jit(solution)/shard_map/ppermute | solution.py:24
  188.1 31.9 %collective-permute-start.13 = (bf16[2,128,2048]{2,1,0:T(8,128)(2,1)S(1)}, bf16[2,128,2048]{2,1,0:T(8,128)(2,1)S(1)}, u32[]{:S(2)}, u32[]{:S(2)}) collective-permute-start(bf16[2,128,2048]{2,1,0:T(8,128)(2,1)S(1)} %collective-permute-done.12), channel_id=1, source_target_pairs={{32,0},{64,32},{96,64},{128,96},{160,128},{192,160},{224,192},{256... | collective-permute-start | bytes 3145736 | tf_op jit(solution)/shard_map/ppermute | solution.py:27
  213.9 112.5 %collective-permute-start.7 = (bf16[2,128,2048]{2,1,0:T(8,128)(2,1)}, bf16[2,128,2048]{2,1,0:T(8,128)(2,1)}, u32[]{:S(2)}, u32[]{:S(2)}) collective-permute-start(bf16[2,128,2048]{2,1,0:T(8,128)(2,1)} %collective-permute-done.6), channel_id=1, source_target_pairs={{0,32},{32,64},{64,96},{96,128},{128,160},{160,192},{192,224},{224... | collective-permute-start | bytes 3145736 | tf_op jit(solution)/shard_map/ppermute | solution.py:24
  220.0 137.6 %collective-permute-start.14 = (bf16[2,128,2048]{2,1,0:T(8,128)(2,1)S(1)}, bf16[2,128,2048]{2,1,0:T(8,128)(2,1)}, u32[]{:S(2)}, u32[]{:S(2)}) collective-permute-start(bf16[2,128,2048]{2,1,0:T(8,128)(2,1)S(1)} %collective-permute-done.13), channel_id=1, source_target_pairs={{32,0},{64,32},{96,64},{128,96},{160,128},{192,160},{224,192},{256... | collective-permute-start | bytes 3145736 | tf_op jit(solution)/shard_map/ppermute | solution.py:27
  373.0 94.0 %copy-start.1 = (bf16[2,256,2048]{2,1,0:T(8,128)(2,1)S(1)}, bf16[2,256,2048]{2,1,0:T(8,128)(2,1)}, u32[]{:S(2)}) copy-start(bf16[2,256,2048]{2,1,0:T(8,128)(2,1)} %param.20) | copy-start | bytes 6291460
Sparse Core Ops, SparseCore 0:
  10.1 78.1 all-gather.9
  94.1 61.4 all-gather.11
  160.3 99.2 reduce-scatter.1
  326.5 55.5 all-gather.13
